TPU v7x, 256 devices: a whole 4x4x8 slice. The times are simulated.
256 devices in a mesh: lon: 16 (over x, y_lo, core), lat: 8 (over z), tm: 2 (over y_hi).
Axes of the slice: x: 4, y: 4 (y_hi: 2, y_lo: 2; y = y_hi * 2 + y_lo), z: 8, core: 2. Of those that a mesh axis runs over, the one named last changes fastest.
Arguments:
- snapshots: float32 [16, 8, 128, 2048], P('tm', None, 'lat', 'lon'), may hold values from -6 to 6
- basis: float32 [64, 8, 128, 2048], P(None, None, 'lat', 'lon'), may hold values from -6 to 6
Outputs:
- new_basis: float32 [64, 8, 128, 2048], P(None, None, 'lat', 'lon')
- coeffs: float32 [64, 16], P(None, 'tm')
All inputs are finite; a program needn't handle non-finite values.
Results may differ from a plain program's by a relative error of at most 0.00011.
Values sent between devices are 32-bit elements; how exact they have to be, the bound alone decides.
No kernel may reach another device: no remote copies, remote signals or barrier semaphores. Data moves between devices by JAX's collectives and lax.ppermute only.
A program may use at most 64 MiB of HBM per device.

v0:
```python
import functools
import math

import jax
import jax.numpy as jnp
from jax import lax
from jax.experimental import pallas as pl
from jax.experimental.pallas import tpu as pltpu
from jax.sharding import Mesh, PartitionSpec as P


SMOOTH_RATE = 0.1
STEP_SIZE = 0.25
SNAPS = 8
LEVELS = 8
ROWS = 16
LANES = 128
EOFS = 64
CELL_ROWS = LEVELS * ROWS
HALF_ROWS = CELL_ROWS // 2
HALF_CELLS = HALF_ROWS * LANES
CHUNK = 8
PAYLOAD = 32
SIDE = PAYLOAD // 2
QROWS = 16
FINAL_ROWS = 16
PART = SNAPS // 2
LON = ("pair", "core")
F32 = jnp.float32
BF16 = jnp.bfloat16
HIGHEST = lax.Precision.HIGHEST
VMEM = pl.BlockSpec(memory_space=pltpu.VMEM)
ANY = pl.BlockSpec(memory_space=pl.ANY)


def lanes_of(shape):
    return lax.broadcasted_iota(jnp.int32, shape, len(shape) - 1)


def shape(*dims, dtype=F32):
    return jax.ShapeDtypeStruct(dims, dtype)


def call(kernel, inputs, outputs, scratch=(), flops=1000000, traffic=1000000, megabytes=8):
    return pl.pallas_call(
        kernel,
        out_shape=outputs,
        in_specs=inputs,
        out_specs=jax.tree.map(lambda _: VMEM, outputs),
        scratch_shapes=scratch,
        cost_estimate=pl.CostEstimate(flops=flops, bytes_accessed=traffic, transcendentals=0),
        compiler_params=pltpu.CompilerParams(vmem_limit_bytes=megabytes << 20),
    )


def pack_kernel(x_ref, packed_ref):
    lane = lanes_of((ROWS, LANES))
    for snap in range(SNAPS):
        packed = jnp.zeros((ROWS, LANES), F32)
        for level in range(LEVELS):
            turned = pltpu.roll(x_ref[snap, level], 16 * level + 3, 1)
            packed = jnp.where((lane >= 16 * level) & (lane < 16 * level + 6), turned, packed)
        packed_ref[pl.ds(ROWS * snap, ROWS), :] = packed


def seam_kernel(x_ref, packed_ref, across_ref, beside_ref, seam_ref, one_ref, two_ref):
    packed = packed_ref[...]
    lane = lanes_of(packed.shape) % 16
    eastern = lax.axis_index("core") == 1
    far, near = across_ref[...] - packed, beside_ref[...] - packed
    west = jnp.where(lane < 3, jnp.where(eastern, near, far), 0.0)
    east = pltpu.roll(jnp.where((lane >= 3) & (lane < 6), jnp.where(eastern, far, near), 0.0), 8, 1)
    seam_ref[...] = west + east
    even = lax.axis_index("lat") % 2 == 0
    for snap in range(SNAPS):
        at = pl.ds(8 * snap, 8)
        low = jnp.swapaxes(x_ref[snap, :, pl.ds(0, 8), :], 0, 1)
        high = jnp.swapaxes(x_ref[snap, :, pl.ds(8, 8), :], 0, 1)
        for row in range(3):
            one_ref[8 * row + snap] = jnp.where(even, high[5 + row], low[row])
            two_ref[8 * row + snap] = jnp.where(even, low[row], high[5 + row])
    low = jnp.swapaxes(jnp.stack([seam_ref[pl.ds(ROWS * snap, 8), :] for snap in range(SNAPS)]), 0, 1)
    high = jnp.swapaxes(jnp.stack([seam_ref[pl.ds(ROWS * snap + 8, 8), :] for snap in range(SNAPS)]), 0, 1)
    for row in range(3):
        one_ref[24 + row] = jnp.where(even, high[5 + row], low[row])
        two_ref[24 + row] = jnp.where(even, low[row], high[5 + row])


def smooth_kernel(begin, x_ref, seam_ref, one_ref, two_ref, order_ref, keep_ref, send_ref, done, seam_edges):
    lat = lax.axis_index("lat")
    even = lat % 2 == 0
    not_first = jnp.where(lat == 0, 0, 1)
    not_last = jnp.where(lat == lax.axis_size("lat") - 1, 0, 1)
    row = lax.broadcasted_iota(jnp.int32, (8, LANES), 0)
    lane = lanes_of((8, LANES))
    inside = jnp.where(row < 4, not_last, not_first) == 1
    zero = jnp.zeros((8, LANES), F32)
    wide_lane = lanes_of((ROWS, LANES))

    def along_rows(field):
        tall = jnp.concatenate(field, axis=0)
        near = pltpu.roll(tall, 1, 0) + pltpu.roll(tall, 23, 0)
        return near[0:8], near[8:16], near[16:24]

    norths = [jnp.where(even, one_ref[24 + i], two_ref[24 + i]) for i in range(3)]
    souths = [jnp.where(even, two_ref[24 + i], one_ref[24 + i]) for i in range(3)]
    seam_edges[...] = jnp.swapaxes(jnp.stack(norths + [zero, zero] + souths), 0, 1)

    def snapshot(snap, carry):
        edges = jnp.swapaxes(
            jnp.stack(
                [jnp.where(even, one_ref[8 * i + snap], two_ref[8 * i + snap]) for i in range(3)]
                + [zero, zero]
                + [jnp.where(even, two_ref[8 * i + snap], one_ref[8 * i + snap]) for i in range(3)]
            ),
            0,
            1,
        )
        fields = [
            (x_ref[snap, level, pl.ds(0, 8), :], x_ref[snap, level, pl.ds(8, 8), :], edges[level])
            for level in range(LEVELS)
        ]
        seam = (
            seam_ref[pl.ds(pl.multiple_of(ROWS * snap, 8), 8), :],
            seam_ref[pl.ds(pl.multiple_of(ROWS * snap + 8, 8), 8), :],
            seam_edges[snap],
        )
        for sweep in range(3):
            tiles = 3 if sweep < 2 else 2
            fresh_fields = []
            for level in range(LEVELS):
                here = fields[level]
                rows = along_rows(here)
                fresh = []
                for tile in range(tiles):
                    near = rows[tile] + pltpu.roll(here[tile], 1, 1) + pltpu.roll(here[tile], LANES - 1, 1)
                    if level > 0:
                        near = near + fields[level - 1][tile]
                    if level < LEVELS - 1:
                        near = near + fields[level + 1][tile]
                    value = here[tile] + SMOOTH_RATE * (near - 6.0 * here[tile])
                    fresh.append(jnp.where(inside, value, 0.0) if tile == 2 else value)
                fresh_fields.append(tuple(fresh))
            rows = along_rows(seam)
            fresh = []
            for tile in range(tiles):
                here = seam[tile]
                near = rows[tile] + pltpu.roll(here, 1, 1) + pltpu.roll(here, LANES - 1, 1)
                near = near + jnp.where(lane >= 16, pltpu.roll(here, 16, 1), 0.0)
                near = near + jnp.where(lane < LANES - 16, pltpu.roll(here, LANES - 16, 1), 0.0)
                value = here + SMOOTH_RATE * (near - 6.0 * here)
                fresh.append(jnp.where(inside, value, 0.0) if tile == 2 else value)
            fields, seam = fresh_fields, tuple(fresh)
        tall_seam = jnp.concatenate(seam, axis=0)
        for level in range(LEVELS):
            first = pltpu.roll(tall_seam, (LANES - 16 * level - 3) % LANES, 1)
            last = pltpu.roll(tall_seam, (117 - 16 * level) % LANES, 1)
            value = jnp.concatenate(fields[level], axis=0)
            value = value + jnp.where(wide_lane < 3, first, jnp.where(wide_lane >= LANES - 3, last, 0.0))
            done[snap - begin, pl.ds(ROWS * level, ROWS), :] = value
        return carry

    lax.fori_loop(begin, begin + PART, snapshot, 0, unroll=2)
    group = lax.axis_index("tm")
    for snap in range(PART):
        keep_ref[snap] = done[snap, pl.ds(pl.multiple_of(HALF_ROWS * group, 8), HALF_ROWS), :]
        send_ref[snap] = done[snap, pl.ds(pl.multiple_of(HALF_ROWS * (1 - group), 8), HALF_ROWS), :]


def pieces(values, count):
    out = []
    for index in range(count):
        piece = values.astype(BF16)
        out.append(piece)
        if index < count - 1:
            values = values - piece.astype(F32)
    return out


def transposed_product(left, right):
    return lax.dot_general(left, right, (((1,), (1,)), ((), ())), preferred_element_type=F32)


def basis_copies(half, q_ref, blocks, sems):
    copies = [
        pltpu.make_async_copy(
            q_ref.at[:, pl.ds(pl.multiple_of(HALF_ROWS * half + QROWS * part, QROWS), QROWS), :],
            blocks.at[part],
            sems.at[part],
        )
        for part in range(HALF_ROWS // QROWS)
    ]
    for copy in copies:
        copy.start()
    return copies


def split_block(block, part, count, stack_ref):
    for sub in range(QROWS // CHUNK):
        turned = jnp.swapaxes(block[:, pl.ds(CHUNK * sub, CHUNK), :], 0, 1)
        for inner in range(CHUNK):
            at = pl.ds(LANES * (QROWS * part + CHUNK * sub + inner), LANES)
            for index, piece in enumerate(pieces(turned[inner], count)):
                stack_ref[pl.ds(EOFS * index, EOFS), at] = piece


def basis_gram_kernel(order_ref, q_ref, stack_ref, gram_ref, blocks, total, sems):
    copies = basis_copies(lax.axis_index("tm"), q_ref, blocks, sems)
    for part, copy in enumerate(copies):
        copy.wait()
        split_block(blocks.at[part], part, 3, stack_ref)
        stack = stack_ref[:, pl.ds(QROWS * LANES * part, QROWS * LANES)]
        product = transposed_product(stack, stack)
        total[...] = product if part == 0 else total[...] + product
    down = total[pl.ds(0, 64), :] + total[pl.ds(64, 64), :] + total[pl.ds(128, 64), :]
    gram_ref[...] = down[:, 0:64] + down[:, 64:128] + down[:, 128:192]


def basis_stack_kernel(order_ref, q_ref, stack_ref, blocks, sems):
    copies = basis_copies(1 - lax.axis_index("tm"), q_ref, blocks, sems)
    for part, copy in enumerate(copies):
        copy.wait()
        split_block(blocks.at[part], part, 2, stack_ref)


def rows_of(refs, at):
    return jnp.concatenate([ref[:, at, :] for ref in refs], axis=0)


def snapshot_columns(refs, start, count):
    turned = jnp.swapaxes(rows_of(refs, pl.ds(start, CHUNK)), 0, 1)
    return [pieces(turned[i], count) for i in range(CHUNK)]


def in_order(mine, other):
    first = lax.axis_index("tm") == 0
    return jnp.where(first, mine, other), jnp.where(first, other, mine)


def own_gram_kernel(stack_ref, one_ref, two_ref, cross_ref, square_ref, pieces_ref, mine_ref):
    mine_ref[pl.ds(0, PART)] = one_ref[...]
    mine_ref[pl.ds(PART, PART)] = two_ref[...]

    def block(step, carry):
        cross, square = carry
        columns = snapshot_columns([mine_ref], pl.multiple_of(CHUNK * step, CHUNK), 3)
        columns = jnp.concatenate([jnp.concatenate(c, axis=0) for c in columns], axis=1)
        width = CHUNK * LANES
        at = pl.ds(pl.multiple_of(width * step, width), width)
        pieces_ref[:, at] = columns
        return cross + transposed_product(stack_ref[:, at], columns), square + transposed_product(columns, columns)

    zeros = (jnp.zeros((192, 24), F32), jnp.zeros((24, 24), F32))
    cross_ref[...], square_ref[...] = lax.fori_loop(0, HALF_ROWS // CHUNK, block, zeros)


def folded(sums, rows):
    down = sums[0:rows] + sums[rows : 2 * rows] + sums[2 * rows : 3 * rows]
    return down[:, 0:8] + down[:, 8:16] + down[:, 16:24]


def snapshot_gram_kernel(
    stack_ref, gram_ref, pieces_ref, other_one_ref, other_two_ref, cross_ref, square_ref, order_ref, own_ref, partner_ref, columns, joined
):
    for step in range(HALF_ROWS // CHUNK):
        other = snapshot_columns([other_one_ref, other_two_ref], CHUNK * step, 3)
        columns[:, pl.ds(CHUNK * LANES * step, CHUNK * LANES)] = jnp.concatenate(
            [jnp.concatenate(c, axis=0) for c in other], axis=1
        )
    cross = transposed_product(stack_ref[...], columns[...])
    square = transposed_product(columns[...], columns[...])
    mixed = transposed_product(pieces_ref[...], columns[...])
    mixed = folded(mixed, 8)
    projection = jnp.concatenate(in_order(folded(cross_ref[...], 64), folded(cross, 64)), axis=1)
    early, late = in_order(folded(square_ref[...], 8), folded(square, 8))
    upper, _ = in_order(mixed, jnp.transpose(mixed))
    square = jnp.concatenate(
        [jnp.concatenate([early, upper], axis=1), jnp.concatenate([jnp.transpose(upper), late], axis=1)], axis=0
    )
    gram = gram_ref[...]
    low, high = gram[0:32, 0:32], gram[32:64, 32:64]
    row = lax.broadcasted_iota(jnp.int32, (32, 32), 0)
    column = lax.broadcasted_iota(jnp.int32, (32, 32), 1)
    diagonal = jnp.sum(jnp.where(row == column, high, 0.0), axis=0, keepdims=True)
    both = jnp.where(row >= column, low, high)
    below = jnp.concatenate(
        [square, jnp.zeros((16, 16), F32), jnp.broadcast_to(diagonal, (16, 32))], axis=1
    )
    right = jnp.concatenate([jnp.transpose(projection), below], axis=0)
    joined[...] = jnp.concatenate([both, gram[32:64, 0:32], right], axis=1)
    core = lax.axis_index("core")
    own_ref[...] = joined[pl.ds(pl.multiple_of(SIDE * core, 8), SIDE), :]
    partner_ref[...] = joined[pl.ds(pl.multiple_of(SIDE * (1 - core), 8), SIDE), :]


def pair_kernel(one_ref, two_ref, out_ref):
    out_ref[...] = jnp.broadcast_to((one_ref[...] + two_ref[...])[None], out_ref.shape)


def group_kernel(parts_ref, out_ref):
    out_ref[...] = jnp.broadcast_to(jnp.sum(parts_ref[...], axis=0)[None], out_ref.shape)


def factor_kernel(cells, parts_ref, maps_ref, coeffs_ref):
    count = parts_ref.shape[0] // 2
    totals = jnp.concatenate(
        [jnp.sum(parts_ref[pl.ds(count * core, count)], axis=0) for core in range(2)], axis=0
    )
    row = lax.broadcasted_iota(jnp.int32, (EOFS, EOFS), 0)
    column = lax.broadcasted_iota(jnp.int32, (EOFS, EOFS), 1)
    both = totals[:, 0:32]
    once = jnp.concatenate(
        [jnp.concatenate([both, jnp.zeros((32, 32), F32)], axis=1), jnp.concatenate([totals[:, 32:64], both], axis=1)], axis=0
    )
    once = jnp.where(((row < 32) & (row > column)) | ((row >= 32) & ((column < 32) | (row < column))), once, 0.0)
    corner = jnp.concatenate([both, jnp.zeros((32, 32), F32)], axis=1)
    diagonal = jnp.concatenate([corner, jnp.broadcast_to(totals[16:17, 64:128], (32, EOFS))], axis=0)
    basis_gram = once + jnp.transpose(once) + jnp.where(row == column, diagonal, 0.0)
    root = math.sqrt(cells)
    coeffs_t = totals[0:16, 64:128] * (1.0 / root)
    snap_gram = totals[16:32, 64:80]
    coeffs_ref[...] = jnp.where(lax.axis_index("tm") == 0, coeffs_t[0:8, :], coeffs_t[8:16, :])
    mixed = (2.0 * STEP_SIZE * root) * coeffs_t + (STEP_SIZE * STEP_SIZE) * jnp.dot(
        snap_gram, coeffs_t, precision=HIGHEST, preferred_element_type=F32
    )
    grown = lax.dot_general(
        coeffs_t, mixed, (((0,), (0,)), ((), ())), precision=HIGHEST, preferred_element_type=F32
    )
    gram = (basis_gram + grown) * (1.0 / cells)
    rows = lax.broadcasted_iota(jnp.int32, (EOFS, EOFS), 0)
    columns = lax.broadcasted_iota(jnp.int32, (EOFS, EOFS), 1)
    work = jnp.concatenate([gram, (rows == columns).astype(F32)], axis=1)
    blocks = [work[8 * i : 8 * i + 8, :] for i in range(8)]
    results = []
    for panel in range(8):
        lower = blocks[panel:]
        columns = [
            [jnp.broadcast_to(b[:, 8 * panel + k : 8 * panel + k + 1], (8, LANES)) for b in lower] for k in range(8)
        ]
        rows = [lower[0][k : k + 1, :] for k in range(8)]
        for k in range(8):
            pivot = columns[k][0][k : k + 1, :]
            if k % 2 == 0:
                corner, upper, side = columns[k + 1][0][k + 1 : k + 2, :], columns[k + 1][0][k : k + 1, :], columns[k][0][k + 1 : k + 2, :]
                inverse = 1.0 / pivot
                following = pivot * (1.0 / (pivot * corner - upper * side))
            else:
                inverse = following
            factors = [c * inverse for c in columns[k]]
            for m in range(k + 1, 8):
                entry = columns[m][0][k : k + 1, :]
                columns[m] = [c - f * entry for c, f in zip(columns[m], factors)]
                rows[m] = rows[m] - factors[0][m : m + 1, :] * rows[k]
            for i in range(panel + 1, 8):
                blocks[i] = blocks[i] - factors[i - panel] * rows[k]
            results.append(rows[k] * lax.rsqrt(pivot))
    inverse = jnp.concatenate(results, axis=0)[:, EOFS:]
    update = lax.dot_general(
        inverse, coeffs_t, (((1,), (1,)), ((), ())), precision=HIGHEST, preferred_element_type=F32
    )
    rows = [
        jnp.concatenate([inverse_part, inverse_part, update_part, update_part], axis=1)
        for inverse_part, update_part in zip(pieces(inverse, 2), pieces(STEP_SIZE * update, 2))
    ]
    maps_ref[...] = jnp.concatenate(rows, axis=0)


def final_kernel(
    maps_ref, near_ref, far_ref, keep_ref, here_one_ref, here_two_ref, send_one_ref, send_two_ref, late_ref, out_ref, blocks, sems
):
    near_refs = (near_ref, [keep_ref], [here_one_ref, here_two_ref])
    far_refs = (far_ref, [send_one_ref, send_two_ref], [late_ref])
    group = lax.axis_index("tm")
    steps = HALF_ROWS // FINAL_ROWS
    copies = []
    for step in range(2 * steps):
        near = step < steps
        half = group if near else 1 - group
        local = step % steps
        stack_ref, mine, other = near_refs if near else far_refs
        for sub in range(FINAL_ROWS // CHUNK):
            start = local * FINAL_ROWS + CHUNK * sub
            at = pl.ds(start, CHUNK)
            early, late = in_order(
                jnp.swapaxes(rows_of(mine, at), 0, 1), jnp.swapaxes(rows_of(other, at), 0, 1)
            )
            columns = jnp.concatenate(
                [
                    jnp.concatenate(pieces(jnp.concatenate([early[i], late[i]], axis=0), 2), axis=0)
                    for i in range(CHUNK)
                ],
                axis=1,
            )
            stack = stack_ref[pl.ds(0, 2 * EOFS), pl.ds(start * LANES, CHUNK * LANES)]
            both = jnp.dot(maps_ref[...], jnp.concatenate([stack, columns], axis=0), preferred_element_type=F32)
            result = both[0:EOFS, :] + both[EOFS:, :]
            result = jnp.stack([result[:, LANES * i : LANES * (i + 1)] for i in range(CHUNK)])
            blocks[step, :, pl.ds(CHUNK * sub, CHUNK), :] = jnp.swapaxes(result, 0, 1)
        to = pl.ds(pl.multiple_of(HALF_ROWS * half + FINAL_ROWS * local, FINAL_ROWS), FINAL_ROWS)
        copy = pltpu.make_async_copy(blocks.at[step], out_ref.at[:, to, :], sems.at[step])
        copy.start()
        copies.append(copy)
    for copy in copies:
        copy.wait()


def swapped(values, axis, first):
    count = lax.axis_size(axis)
    pairs = [(i, (i + 1) % count) for i in range(first, count - first % 2 * (axis == "lat"), 2)]
    return lax.ppermute(values, axis, [p for one, two in pairs for p in ((one, two), (two, one))])


def across(values, axis):
    return lax.ppermute(values, axis, [(0, 1), (1, 0)])


def gathered(values, axes):
    return lax.all_to_all(values, axes, 0, 0)


def update(snapshots, basis):
    lat_count = lax.axis_size("lat")
    cells = CELL_ROWS * LANES * lat_count * lax.axis_size(LON)
    q = pltpu.with_memory_space_constraint(basis.reshape(EOFS, CELL_ROWS, LANES), pltpu.HBM)

    packed = call(pack_kernel, [VMEM], shape(CELL_ROWS, LANES))(snapshots)
    chip = swapped(packed, LON, 1)
    beside = across(packed, "core")
    seam, one, two = call(
        seam_kernel, [VMEM] * 4, (shape(CELL_ROWS, LANES), shape(27, 8, LANES), shape(27, 8, LANES))
    )(snapshots, packed, chip, beside)
    one, two = swapped(one, "lat", 0), swapped(two, "lat", 1)
    parts = HALF_ROWS // QROWS
    stack, gram = call(
        basis_gram_kernel,
        [VMEM, ANY],
        (shape(3 * EOFS, HALF_CELLS, dtype=BF16), shape(EOFS, EOFS)),
        [pltpu.VMEM((parts, EOFS, QROWS, LANES), F32), pltpu.VMEM((192, 192), F32), pltpu.SemaphoreType.DMA((parts,))],
        traffic=8 << 20,
    )(seam, q)
    far = call(
        basis_stack_kernel,
        [VMEM, ANY],
        shape(2 * EOFS, HALF_CELLS, dtype=BF16),
        [pltpu.VMEM((parts, EOFS, QROWS, LANES), F32), pltpu.SemaphoreType.DMA((parts,))],
        traffic=6 << 20,
    )(gram, q)
    order, keep, send, here = far, [], [], []
    for begin in (0, PART):
        kept, sent = call(
            functools.partial(smooth_kernel, begin),
            [VMEM] * 5,
            (shape(PART, HALF_ROWS, LANES),) * 2,
            [pltpu.VMEM((PART, CELL_ROWS, LANES), F32), pltpu.VMEM((SNAPS, 8, LANES), F32)],
        )(snapshots, seam, one, two, order)
        here.append(across(sent, "tm"))
        order = kept
        keep.append(kept)
        send.append(sent)
    cross, square, split, keep = call(
        own_gram_kernel,
        [VMEM] * 3,
        (shape(192, 24), shape(24, 24), shape(24, HALF_CELLS, dtype=BF16), shape(SNAPS, HALF_ROWS, LANES)),
        traffic=4 << 20,
    )(stack, *keep)
    side = shape(SIDE, LANES)
    late = across(keep, "tm")
    mine, theirs = call(
        snapshot_gram_kernel, [VMEM] * 8, (side, side), [pltpu.VMEM((24, HALF_CELLS), BF16), pltpu.VMEM((PAYLOAD, LANES), F32)]
    )(stack, gram, split, *here, cross, square, far)
    group = lax.axis_size(("pair", "tm"))
    spread = call(pair_kernel, [VMEM] * 2, shape(group, SIDE, LANES))(mine, across(theirs, "core"))
    spread = gathered(spread, ("pair", "tm"))
    spread = call(group_kernel, [VMEM], shape(2 * lat_count, SIDE, LANES))(spread)
    spread = gathered(spread, ("core", "lat"))
    maps, coeffs_t = call(
        functools.partial(factor_kernel, cells), [VMEM], (shape(2 * EOFS, 160, dtype=BF16), shape(SNAPS, EOFS))
    )(spread)
    final_steps = CELL_ROWS // FINAL_ROWS
    new_basis = pl.pallas_call(
        final_kernel,
        out_shape=shape(EOFS, CELL_ROWS, LANES),
        in_specs=[VMEM] * 9,
        out_specs=ANY,
        scratch_shapes=[
            pltpu.VMEM((final_steps, EOFS, FINAL_ROWS, LANES), F32),
            pltpu.SemaphoreType.DMA((final_steps,)),
        ],
        compiler_params=pltpu.CompilerParams(vmem_limit_bytes=8 << 20),
    )(maps, stack, far, keep, *here, *send, late)
    return (new_basis.reshape(basis.shape), coeffs_t.T)


def solution(mesh):
    pairs = mesh.shape["lon"] // 2
    split = Mesh(mesh.devices.reshape(pairs, 2, *mesh.devices.shape[1:]), LON + tuple(mesh.axis_names[1:]))
    fields = P(None, None, "lat", LON)
    return jax.shard_map(
        update,
        mesh=split,
        in_specs=(P("tm", None, "lat", LON), fields),
        out_specs=(fields, P(None, "tm")),
        check_vma=False,
    )
```

profile of v0, /device:TPU:1, one launch (start us, length us, event | category | flops | bytes accessed | tf_op | source)
XLA Modules:
  0.0 72.5 jit_solution(15806232187855032842)
XLA Ops:
  0.6 1.0 %copy-done.2 = f32[8,8,16,128]{3,2,1,0:T(8,128)S(1)} copy-done((f32[8,8,16,128]{3,2,1,0:T(8,128)S(1)}, f32[8,8,16,128]{3,2,1,0:T(8,128)}, u32[]{:S(2)}) %copy-start.2) | copy-done | bytes 524312
  1.7 0.2 shard_map.41.packed_ref
  1.9 3.3 %collective-permute-start.1 = (f32[128,128]{1,0:T(8,128)S(1)}, f32[128,128]{1,0:T(8,128)S(1)}, u32[]{:S(2)}, u32[]{:S(2)}) collective-permute-start(f32[128,128]{1,0:T(8,128)S(1)} %shard_map.41.packed_ref), channel_id=1, source_target_pairs={{0,16},{16,0},{1,17},{17,1},{2,18},{18,2},{3,19},{19,3},{4,20},{20... | collective-permute-start | bytes 196616 | tf_op jit(solution)/shard_map/ppermute | solution.py:414
  5.2 0.9 %collective-permute-done.1.beside_ref = f32[128,128]{1,0:T(8,128)S(1)} collective-permute-done((f32[128,128]{1,0:T(8,128)S(1)}, f32[128,128]{1,0:T(8,128)S(1)}, u32[]{:S(2)}, u32[]{:S(2)}) %collective-permute-start.1) | collective-permute-done | bytes 65568 | tf_op jit(solution)/shard_map/ppermute | solution.py:414
  6.1 2.8 %collective-permute-done.across_ref = f32[128,128]{1,0:T(8,128)S(1)} collective-permute-done((f32[128,128]{1,0:T(8,128)S(1)}, f32[128,128]{1,0:T(8,128)S(1)}, u32[]{:S(2)}, u32[]{:S(2)}) %collective-permute-start) | collective-permute-done | bytes 65568 | tf_op jit(solution)/shard_map/ppermute | solution.py:410
  9.1 0.7 collective-permute-start.3
  9.7 3.6 %shard_map.43 = (bf16[192,8192]{1,0:T(8,128)(2,1)S(1)}, f32[64,64]{1,0:T(8,128)S(1)}) custom-call(f32[128,128]{1,0:T(8,128)S(1)} %get-tuple-element.19.order_ref.seam_ref, f32[64,128,128]{2,1,0:T(8,128)} %bitcast.3), custom_call_target="tpu_custom_call" | custom-call | flops 1000000 | bytes 8388608 | tf_op jit(solution)/shard_map/pallas_call | solution.py:434
  13.4 2.9 %shard_map.44.order_ref.far_ref = bf16[128,8192]{1,0:T(8,128)(2,1)S(1)} custom-call(f32[64,64]{1,0:T(8,128)S(1)} %get-tuple-element.21.order_ref.gram_ref, f32[64,128,128]{2,1,0:T(8,128)} %bitcast.4), custom_call_target="tpu_custom_call" | custom-call | flops 1000000 | bytes 6291456 | tf_op jit(solution)/shard_map/pallas_call | solution.py:441
  16.3 1.4 %shard_map.45 = (f32[4,64,128]{2,1,0:T(8,128)S(1)}, f32[4,64,128]{2,1,0:T(8,128)S(1)}) custom-call(f32[8,8,16,128]{3,2,1,0:T(8,128)S(1)} %copy-done.3, f32[128,128]{1,0:T(8,128)S(1)} %get-tuple-element.19.order_ref.seam_ref, f32[27,8,128]{2,1,0:T(8,128)S(1)} %collective-permute-done.2.one_ref, f32[27,8,128]{2,1,0:T(8,128)S(1)} %collective-permute-done.3.two_ref, ...), custom_call_target="tpu_custom_call" | custom-call | flops 1000000 | bytes 1000000 | tf_op jit(solution)/shard_map/pallas_call | solution.py:450
  17.7 1.4 %shard_map.46 = (f32[4,64,128]{2,1,0:T(8,128)S(1)}, f32[4,64,128]{2,1,0:T(8,128)S(1)}) custom-call(f32[8,8,16,128]{3,2,1,0:T(8,128)S(1)} %copy-done.3, f32[128,128]{1,0:T(8,128)S(1)} %get-tuple-element.19.order_ref.seam_ref, f32[27,8,128]{2,1,0:T(8,128)S(1)} %collective-permute-done.2.one_ref, f32[27,8,128]{2,1,0:T(8,128)S(1)} %collective-permute-done.3.two_ref, ...), custom_call_target="tpu_custom_call" | custom-call | flops 1000000 | bytes 1000000 | tf_op jit(solution)/shard_map/pallas_call | solution.py:450
  19.1 2.9 %collective-permute-start.5 = (f32[4,64,128]{2,1,0:T(8,128)S(1)}, f32[4,64,128]{2,1,0:T(8,128)S(1)}, u32[]{:S(2)}, u32[]{:S(2)}) collective-permute-start(f32[4,64,128]{2,1,0:T(8,128)S(1)} %get-tuple-element.28.send_two_ref), channel_id=1, source_target_pairs={{0,1},{1,0},{2,3},{3,2},{4,5},{5,4},{6,7},{7,6},{8,9},{9,8},{10,11... | collective-permute-start | bytes 393224 | tf_op jit(solution)/shard_map/ppermute | solution.py:414
  22.2 2.2 %shard_map.47 = (f32[192,24]{1,0:T(8,128)S(1)}, f32[24,24]{1,0:T(8,128)S(1)}, bf16[24,8192]{1,0:T(8,128)(2,1)S(1)}, f32[8,64,128]{2,1,0:T(8,128)S(1)}) custom-call(bf16[192,8192]{1,0:T(8,128)(2,1)S(1)} %get-tuple-element.20.stack_ref.near_ref, f32[4,64,128]{2,1,0:T(8,128)S(1)} %get-tuple-element.24.order_ref.one_ref, f32[4,64,128]{2,1,0:T(8,128)S(1)} %get-tuple-element.25.two_ref), custom_call_target="tpu_custom_call" | custom-call | flops 1000000 | bytes 4194304 | tf_op jit(solution)/shard_map/pallas_call | solution.py:460
  24.5 4.5 %collective-permute-done.4.other_one_ref.here_one_ref = f32[4,64,128]{2,1,0:T(8,128)S(1)} collective-permute-done((f32[4,64,128]{2,1,0:T(8,128)S(1)}, f32[4,64,128]{2,1,0:T(8,128)S(1)}, u32[]{:S(2)}, u32[]{:S(2)}) %collective-permute-start.4) | collective-permute-done | bytes 131104 | tf_op jit(solution)/shard_map/ppermute | solution.py:414
  29.0 1.5 %shard_map.48 = (f32[16,128]{1,0:T(8,128)S(1)}, f32[16,128]{1,0:T(8,128)S(1)}) custom-call(bf16[192,8192]{1,0:T(8,128)(2,1)S(1)} %get-tuple-element.20.stack_ref.near_ref, f32[64,64]{1,0:T(8,128)S(1)} %get-tuple-element.21.order_ref.gram_ref, bf16[24,8192]{1,0:T(8,128)(2,1)S(1)} %get-tuple-element.26.pieces_ref, ...), custom_call_target="tpu_custom_call" | custom-call | flops 1000000 | bytes 1000000 | tf_op jit(solution)/shard_map/pallas_call | solution.py:468
  30.6 2.3 %collective-permute-start.6 = (f32[16,128]{1,0:T(8,128)S(1)}, f32[16,128]{1,0:T(8,128)S(1)}, u32[]{:S(2)}, u32[]{:S(2)}) collective-permute-start(f32[16,128]{1,0:T(8,128)S(1)} %get-tuple-element.32), channel_id=1, source_target_pairs={{0,16},{16,0},{1,17},{17,1},{2,18},{18,2},{3,19},{19,3},{4,20},{20... | collective-permute-start | bytes 24584 | tf_op jit(solution)/shard_map/ppermute | solution.py:414
  32.9 0.8 %collective-permute-done.6.two_ref = f32[16,128]{1,0:T(8,128)S(1)} collective-permute-done((f32[16,128]{1,0:T(8,128)S(1)}, f32[16,128]{1,0:T(8,128)S(1)}, u32[]{:S(2)}, u32[]{:S(2)}) %collective-permute-start.6) | collective-permute-done | bytes 8224 | tf_op jit(solution)/shard_map/ppermute | solution.py:414
  33.7 0.7 shard_map.49
  34.4 5.5 %all-to-all-start = ((f32[16,16,128]{2,1,0:T(8,128)}), f32[16,16,128]{2,1,0:T(8,128)S(1)}, u32[]{:S(2)}, u32[]{:S(2)}) async-start(f32[16,16,128]{2,1,0:T(8,128)} %shard_map.49), calls=%async_computation | async-start | bytes 262144 | tf_op jit(solution)/shard_map/all_to_all | solution.py:418
  39.9 2.9 %collective-permute-start.7 = (f32[8,64,128]{2,1,0:T(8,128)S(1)}, f32[8,64,128]{2,1,0:T(8,128)S(1)}, u32[]{:S(2)}, u32[]{:S(2)}) collective-permute-start(f32[8,64,128]{2,1,0:T(8,128)S(1)} %get-tuple-element.34.keep_ref), channel_id=1, source_target_pairs={{0,1},{1,0},{2,3},{3,2},{4,5},{5,4},{6,7},{7,6},{8,9},{9,8},{10,11... | collective-permute-start | bytes 786440 | tf_op jit(solution)/shard_map/ppermute | solution.py:414
  42.8 4.2 %all-to-all-done.parts_ref = f32[16,16,128]{2,1,0:T(8,128)S(1)} async-done(((f32[16,16,128]{2,1,0:T(8,128)}), f32[16,16,128]{2,1,0:T(8,128)S(1)}, u32[]{:S(2)}, u32[]{:S(2)}) %all-to-all-start) | async-done | bytes 131104 | tf_op jit(solution)/shard_map/all_to_all | solution.py:418
  47.0 18.1 %all_to_all.10.parts_ref = f32[16,16,128]{2,1,0:T(8,128)S(1)} all-to-all(f32[16,16,128]{2,1,0:T(8,128)S(1)} %shard_map.50), channel_id=1, replica_groups=mesh['pair'=8,'core'=2,'lat'=8,'tm'=2] {'core','lat'}, dimensions={0} | all-to-all | bytes 262144 | tf_op jit(solution)/shard_map/all_to_all | solution.py:418
  65.1 2.9 %shard_map.51 = (bf16[128,160]{1,0:T(8,128)(2,1)S(1)}, f32[8,64]{1,0:T(8,128)}) custom-call(f32[16,16,128]{2,1,0:T(8,128)S(1)} %all_to_all.10.parts_ref), custom_call_target="tpu_custom_call" | custom-call | flops 1000000 | bytes 1000000 | tf_op jit(solution)/shard_map/pallas_call | solution.py:476
  68.0 1.9 %copy-done.1 = bf16[192,8192]{1,0:T(8,128)(2,1)S(1)} copy-done((bf16[192,8192]{1,0:T(8,128)(2,1)S(1)}, bf16[192,8192]{1,0:T(8,128)(2,1)}, u32[]{:S(2)}) %copy-start.1) | copy-done | bytes 3145752
  69.9 2.4 %shard_map.52 = f32[64,128,128]{2,1,0:T(8,128)} custom-call(bf16[128,160]{1,0:T(8,128)(2,1)S(1)} %get-tuple-element.33.maps_ref, bf16[192,8192]{1,0:T(8,128)(2,1)S(1)} %copy-done.1, bf16[128,8192]{1,0:T(8,128)(2,1)S(1)} %shard_map.44.order_ref.far_ref, f32[8,64,128]{2,1,0:T(8,128)S(1)} %get-tuple-element.34.keep_ref, ...), custom_call_target="tpu_custom_call" | custom-call | tf_op jit(solution)/shard_map/pallas_call | solution.py:480
  (15 shorter events, 0.5 us)
Async XLA Ops:
  0.6 1.0 %copy-start.2 = (f32[8,8,16,128]{3,2,1,0:T(8,128)S(1)}, f32[8,8,16,128]{3,2,1,0:T(8,128)}, u32[]{:S(2)}) copy-start(f32[8,8,16,128]{3,2,1,0:T(8,128)} %x_ref.7) | copy-start | bytes 1572868
  1.9 4.2 %collective-permute-start.1 = (f32[128,128]{1,0:T(8,128)S(1)}, f32[128,128]{1,0:T(8,128)S(1)}, u32[]{:S(2)}, u32[]{:S(2)}) collective-permute-start(f32[128,128]{1,0:T(8,128)S(1)} %shard_map.41.packed_ref), channel_id=1, source_target_pairs={{0,16},{16,0},{1,17},{17,1},{2,18},{18,2},{3,19},{19,3},{4,20},{20... | collective-permute-start | bytes 196616 | tf_op jit(solution)/shard_map/ppermute | solution.py:414
  5.2 3.7 %collective-permute-start = (f32[128,128]{1,0:T(8,128)S(1)}, f32[128,128]{1,0:T(8,128)S(1)}, u32[]{:S(2)}, u32[]{:S(2)}) collective-permute-start(f32[128,128]{1,0:T(8,128)S(1)} %shard_map.41.packed_ref), channel_id=1, source_target_pairs={{16,32},{32,16},{48,64},{64,48},{80,96},{96,80},{112,128},{128,112... | collective-permute-start | bytes 196616 | tf_op jit(solution)/shard_map/ppermute | solution.py:410
  9.0 7.4 %collective-permute-start.2 = (f32[27,8,128]{2,1,0:T(8,128)S(1)}, f32[27,8,128]{2,1,0:T(8,128)S(1)}, u32[]{:S(2)}, u32[]{:S(2)}) collective-permute-start(f32[27,8,128]{2,1,0:T(8,128)S(1)} %get-tuple-element.22), channel_id=1, source_target_pairs={{0,2},{2,0},{4,6},{6,4},{8,10},{10,8},{12,14},{14,12},{1,3},{3,1},... | collective-permute-start | bytes 331784 | tf_op jit(solution)/shard_map/ppermute | solution.py:410
  9.1 7.3 %collective-permute-start.3 = (f32[27,8,128]{2,1,0:T(8,128)S(1)}, f32[27,8,128]{2,1,0:T(8,128)S(1)}, u32[]{:S(2)}, u32[]{:S(2)}) collective-permute-start(f32[27,8,128]{2,1,0:T(8,128)S(1)} %get-tuple-element.23), channel_id=1, source_target_pairs={{2,4},{4,2},{6,8},{8,6},{10,12},{12,10},{3,5},{5,3},{7,9},{9,7},{1... | collective-permute-start | bytes 331784 | tf_op jit(solution)/shard_map/ppermute | solution.py:410
  13.3 15.7 %copy-start = (bf16[192,8192]{1,0:T(8,128)(2,1)}, bf16[192,8192]{1,0:T(8,128)(2,1)S(1)}, u32[]{:S(2)}) copy-start(bf16[192,8192]{1,0:T(8,128)(2,1)S(1)} %get-tuple-element.20.stack_ref.near_ref) | copy-start | bytes 9437188
  13.4 3.0 %copy-start.3 = (f32[8,8,16,128]{3,2,1,0:T(8,128)S(1)}, f32[8,8,16,128]{3,2,1,0:T(8,128)}, u32[]{:S(2)}) copy-start(f32[8,8,16,128]{3,2,1,0:T(8,128)} %x_ref.7) | copy-start | bytes 1572868
  19.1 5.4 %collective-permute-start.5 = (f32[4,64,128]{2,1,0:T(8,128)S(1)}, f32[4,64,128]{2,1,0:T(8,128)S(1)}, u32[]{:S(2)}, u32[]{:S(2)}) collective-permute-start(f32[4,64,128]{2,1,0:T(8,128)S(1)} %get-tuple-element.28.send_two_ref), channel_id=1, source_target_pairs={{0,1},{1,0},{2,3},{3,2},{4,5},{5,4},{6,7},{7,6},{8,9},{9,8},{10,11... | collective-permute-start | bytes 393224 | tf_op jit(solution)/shard_map/ppermute | solution.py:414
  22.0 7.0 %collective-permute-start.4 = (f32[4,64,128]{2,1,0:T(8,128)S(1)}, f32[4,64,128]{2,1,0:T(8,128)S(1)}, u32[]{:S(2)}, u32[]{:S(2)}) collective-permute-start(f32[4,64,128]{2,1,0:T(8,128)S(1)} %get-tuple-element.27.send_one_ref), channel_id=1, source_target_pairs={{0,1},{1,0},{2,3},{3,2},{4,5},{5,4},{6,7},{7,6},{8,9},{9,8},{10,11... | collective-permute-start | bytes 393224 | tf_op jit(solution)/shard_map/ppermute | solution.py:414
  30.6 3.2 %collective-permute-start.6 = (f32[16,128]{1,0:T(8,128)S(1)}, f32[16,128]{1,0:T(8,128)S(1)}, u32[]{:S(2)}, u32[]{:S(2)}) collective-permute-start(f32[16,128]{1,0:T(8,128)S(1)} %get-tuple-element.32), channel_id=1, source_target_pairs={{0,16},{16,0},{1,17},{17,1},{2,18},{18,2},{3,19},{19,3},{4,20},{20... | collective-permute-start | bytes 24584 | tf_op jit(solution)/shard_map/ppermute | solution.py:414
  34.4 12.6 %all-to-all-start = ((f32[16,16,128]{2,1,0:T(8,128)}), f32[16,16,128]{2,1,0:T(8,128)S(1)}, u32[]{:S(2)}, u32[]{:S(2)}) async-start(f32[16,16,128]{2,1,0:T(8,128)} %shard_map.49), calls=%async_computation | async-start | bytes 262144 | tf_op jit(solution)/shard_map/all_to_all | solution.py:418
  39.9 28.1 %collective-permute-start.7 = (f32[8,64,128]{2,1,0:T(8,128)S(1)}, f32[8,64,128]{2,1,0:T(8,128)S(1)}, u32[]{:S(2)}, u32[]{:S(2)}) collective-permute-start(f32[8,64,128]{2,1,0:T(8,128)S(1)} %get-tuple-element.34.keep_ref), channel_id=1, source_target_pairs={{0,1},{1,0},{2,3},{3,2},{4,5},{5,4},{6,7},{7,6},{8,9},{9,8},{10,11... | collective-permute-start | bytes 786440 | tf_op jit(solution)/shard_map/ppermute | solution.py:414
  68.0 1.9 %copy-start.1 = (bf16[192,8192]{1,0:T(8,128)(2,1)S(1)}, bf16[192,8192]{1,0:T(8,128)(2,1)}, u32[]{:S(2)}) copy-start(bf16[192,8192]{1,0:T(8,128)(2,1)} %copy-done) | copy-start | bytes 9437188
where the time goes:
time: 72.9 us; the launch traced here: 72.5 us
  Pallas kernels  19.4 us (27%)
  blocking collectives  18.1 us (25%)
  starting transfers between devices  17.8 us (24%)
  waiting for transfers between devices  13.3 us (18%)
  local copies, waits for them, and re-layouts  2.94 us (4%)
  between operations  0.92 us (1%)
    all_to_all x1, blocking collectives, gathered(): return lax.all_to_all(values, axes, 0, 0)  18.1 us
    ppermute x5, starting transfers between devices, across(): return lax.ppermute(values, axis, [(0, 1), (1, 0)])  11.6 us
    ppermute x5, waiting for transfers between devices, across(): return lax.ppermute(values, axis, [(0, 1), (1, 0)])  6.34 us
    all_to_all x1, starting transfers between devices, gathered(): return lax.all_to_all(values, axes, 0, 0)  5.53 us
    all_to_all x1, waiting for transfers between devices, gathered(): return lax.all_to_all(values, axes, 0, 0)  4.2 us
    pallas_call x1, Pallas kernels, update(): call(basis_gram_kernel, [VMEM, ANY], (shape(3 * EOFS, HALF_CELLS, dtype=B...  3.6 us
    pallas_call x1, Pallas kernels, update(): call(basis_stack_kernel, [VMEM, ANY], shape(2 * EOFS, HALF_CELLS, dtype=B...  2.94 us
    pallas_call x1, Pallas kernels, update(): call(functools.partial(factor_kernel, cells), [VMEM], (shape(2 * EOFS, 16...  2.94 us
  transfers between devices with their start and end apart: 9, of which 6 were waited for; matrix products, arithmetic and copies ran while one was open for 0% of the time, Pallas kernels for 16%

commit v1 on v0

--- a/solution.py
+++ b/solution.py
@@ -63,7 +63,7 @@
         packed_ref[pl.ds(ROWS * snap, ROWS), :] = packed
 
 
-def seam_kernel(x_ref, packed_ref, across_ref, beside_ref, seam_ref, one_ref, two_ref):
+def seam_kernel(x_ref, packed_ref, across_ref, beside_ref, order_ref, seam_ref, one_ref, two_ref):
     packed = packed_ref[...]
     lane = lanes_of(packed.shape) % 16
     eastern = lax.axis_index("core") == 1
@@ -426,11 +426,18 @@
     packed = call(pack_kernel, [VMEM], shape(CELL_ROWS, LANES))(snapshots)
     chip = swapped(packed, LON, 1)
     beside = across(packed, "core")
+    parts = HALF_ROWS // QROWS
+    far = call(
+        basis_stack_kernel,
+        [VMEM, ANY],
+        shape(2 * EOFS, HALF_CELLS, dtype=BF16),
+        [pltpu.VMEM((parts, EOFS, QROWS, LANES), F32), pltpu.SemaphoreType.DMA((parts,))],
+        traffic=6 << 20,
+    )(packed, q)
     seam, one, two = call(
-        seam_kernel, [VMEM] * 4, (shape(CELL_ROWS, LANES), shape(27, 8, LANES), shape(27, 8, LANES))
-    )(snapshots, packed, chip, beside)
+        seam_kernel, [VMEM] * 5, (shape(CELL_ROWS, LANES), shape(27, 8, LANES), shape(27, 8, LANES))
+    )(snapshots, packed, chip, beside, far)
     one, two = swapped(one, "lat", 0), swapped(two, "lat", 1)
-    parts = HALF_ROWS // QROWS
     stack, gram = call(
         basis_gram_kernel,
         [VMEM, ANY],
@@ -438,14 +445,7 @@
         [pltpu.VMEM((parts, EOFS, QROWS, LANES), F32), pltpu.VMEM((192, 192), F32), pltpu.SemaphoreType.DMA((parts,))],
         traffic=8 << 20,
     )(seam, q)
-    far = call(
-        basis_stack_kernel,
-        [VMEM, ANY],
-        shape(2 * EOFS, HALF_CELLS, dtype=BF16),
-        [pltpu.VMEM((parts, EOFS, QROWS, LANES), F32), pltpu.SemaphoreType.DMA((parts,))],
-        traffic=6 << 20,
-    )(gram, q)
-    order, keep, send, here = far, [], [], []
+    order, keep, send, here = gram, [], [], []
     for begin in (0, PART):
         kept, sent = call(
             functools.partial(smooth_kernel, begin),

time: 72.9 us -> 72.1 us (0.989)
  blocking collectives: 18.1 us -> 20.3 us
  waiting for transfers between devices: 13.3 us -> 11.2 us
  Pallas kernels: 19.4 us -> 18.3 us
    all_to_all x1, blocking collectives: 18.1 us -> 20.3 us  [gathered(): return lax.all_to_all(values, axes, 0, 0)]
    ppermute x5, waiting for transfers between devices: 6.34 us -> 5.2 us  [across(): return lax.ppermute(values, axis, [(0, 1), (1, 0)])]
    pallas_call x1, Pallas kernels: 2.94 us -> 1.86 us  [update(): call(basis_stack_kernel, [VMEM, ANY], shape(2 * EOFS, HALF_CELLS, dtype=B...]
    ppermute x3, waiting for transfers between devices: 2.79 us -> 1.82 us  [swapped(): lax.ppermute(values, axis, [p for one, two in pairs for p in ((one, two),...]
  transfers between devices with their start and end apart: 9 -> 9, of which waited for: 6 -> 5; matrix products, arithmetic and copies ran while one was open for 0% -> 0% of each run, Pallas kernels for 16% -> 15%
where the time goes in v1:
time: 72.1 us; the launch traced here: 71.7 us
  blocking collectives  20.3 us (28%)
  Pallas kernels  18.3 us (25%)
  starting transfers between devices  18.1 us (25%)
  waiting for transfers between devices  11.2 us (16%)
  local copies, waits for them, and re-layouts  2.93 us (4%)
  between operations  0.93 us (1%)
    all_to_all x1, blocking collectives, gathered(): return lax.all_to_all(values, axes, 0, 0)  20.3 us
    ppermute x5, starting transfers between devices, across(): return lax.ppermute(values, axis, [(0, 1), (1, 0)])  11.8 us
    all_to_all x1, starting transfers between devices, gathered(): return lax.all_to_all(values, axes, 0, 0)  5.53 us
    ppermute x5, waiting for transfers between devices, across(): return lax.ppermute(values, axis, [(0, 1), (1, 0)])  5.2 us
    all_to_all x1, waiting for transfers between devices, gathered(): return lax.all_to_all(values, axes, 0, 0)  4.2 us
    pallas_call x1, Pallas kernels, update(): call(basis_gram_kernel, [VMEM, ANY], (shape(3 * EOFS, HALF_CELLS, dtype=B...  3.6 us
    pallas_call x1, Pallas kernels, update(): call(functools.partial(factor_kernel, cells), [VMEM], (shape(2 * EOFS, 16...  2.94 us
    unnamed x8, local copies, waits for them, and re-layouts  2.93 us
  transfers between devices with their start and end apart: 9, of which 5 were waited for; matrix products, arithmetic and copies ran while one was open for 0% of the time, Pallas kernels for 15%

profile of v1, /device:TPU:1, one launch (start us, length us, event | category | flops | bytes accessed | tf_op | source)
XLA Modules:
  0.0 71.7 jit_solution(15381525089247461302)
XLA Ops:
  0.6 1.0 %copy-done.2 = f32[8,8,16,128]{3,2,1,0:T(8,128)S(1)} copy-done((f32[8,8,16,128]{3,2,1,0:T(8,128)S(1)}, f32[8,8,16,128]{3,2,1,0:T(8,128)}, u32[]{:S(2)}) %copy-start.2) | copy-done | bytes 524312
  1.7 0.2 shard_map.41.order_ref.packed_ref
  1.9 3.3 %collective-permute-start.1 = (f32[128,128]{1,0:T(8,128)S(1)}, f32[128,128]{1,0:T(8,128)S(1)}, u32[]{:S(2)}, u32[]{:S(2)}) collective-permute-start(f32[128,128]{1,0:T(8,128)S(1)} %shard_map.41.order_ref.packed_ref), channel_id=1, source_target_pairs={{0,16},{16,0},{1,17},{17,1},{2,18},{18,2},{3,19},{19,3},{4,20},{20... | collective-permute-start | bytes 196616 | tf_op jit(solution)/shard_map/ppermute | solution.py:414
  5.2 1.9 %shard_map.42.order_ref.far_ref = bf16[128,8192]{1,0:T(8,128)(2,1)S(1)} custom-call(f32[128,128]{1,0:T(8,128)S(1)} %shard_map.41.order_ref.packed_ref, f32[64,128,128]{2,1,0:T(8,128)} %bitcast.3), custom_call_target="tpu_custom_call" | custom-call | flops 1000000 | bytes 6291456 | tf_op jit(solution)/shard_map/pallas_call | solution.py:430
  7.0 1.8 %collective-permute-done.across_ref = f32[128,128]{1,0:T(8,128)S(1)} collective-permute-done((f32[128,128]{1,0:T(8,128)S(1)}, f32[128,128]{1,0:T(8,128)S(1)}, u32[]{:S(2)}, u32[]{:S(2)}) %collective-permute-start) | collective-permute-done | bytes 65568 | tf_op jit(solution)/shard_map/ppermute | solution.py:410
  9.1 0.7 collective-permute-start.3
  9.7 3.6 %shard_map.44 = (bf16[192,8192]{1,0:T(8,128)(2,1)S(1)}, f32[64,64]{1,0:T(8,128)S(1)}) custom-call(f32[128,128]{1,0:T(8,128)S(1)} %get-tuple-element.19.order_ref.seam_ref, f32[64,128,128]{2,1,0:T(8,128)} %bitcast.4), custom_call_target="tpu_custom_call" | custom-call | flops 1000000 | bytes 8388608 | tf_op jit(solution)/shard_map/pallas_call | solution.py:441
  13.4 1.4 %shard_map.45 = (f32[4,64,128]{2,1,0:T(8,128)S(1)}, f32[4,64,128]{2,1,0:T(8,128)S(1)}) custom-call(f32[8,8,16,128]{3,2,1,0:T(8,128)S(1)} %copy-done.3, f32[128,128]{1,0:T(8,128)S(1)} %get-tuple-element.19.order_ref.seam_ref, f32[27,8,128]{2,1,0:T(8,128)S(1)} %collective-permute-done.2.one_ref, f32[27,8,128]{2,1,0:T(8,128)S(1)} %collective-permute-done.3.two_ref, ...), custom_call_target="tpu_custom_call" | custom-call | flops 1000000 | bytes 1000000 | tf_op jit(solution)/shard_map/pallas_call | solution.py:450
  14.8 1.4 %shard_map.46 = (f32[4,64,128]{2,1,0:T(8,128)S(1)}, f32[4,64,128]{2,1,0:T(8,128)S(1)}) custom-call(f32[8,8,16,128]{3,2,1,0:T(8,128)S(1)} %copy-done.3, f32[128,128]{1,0:T(8,128)S(1)} %get-tuple-element.19.order_ref.seam_ref, f32[27,8,128]{2,1,0:T(8,128)S(1)} %collective-permute-done.2.one_ref, f32[27,8,128]{2,1,0:T(8,128)S(1)} %collective-permute-done.3.two_ref, ...), custom_call_target="tpu_custom_call" | custom-call | flops 1000000 | bytes 1000000 | tf_op jit(solution)/shard_map/pallas_call | solution.py:450
  16.2 2.9 %collective-permute-start.5 = (f32[4,64,128]{2,1,0:T(8,128)S(1)}, f32[4,64,128]{2,1,0:T(8,128)S(1)}, u32[]{:S(2)}, u32[]{:S(2)}) collective-permute-start(f32[4,64,128]{2,1,0:T(8,128)S(1)} %get-tuple-element.28.send_two_ref), channel_id=1, source_target_pairs={{0,1},{1,0},{2,3},{3,2},{4,5},{5,4},{6,7},{7,6},{8,9},{9,8},{10,11... | collective-permute-start | bytes 393224 | tf_op jit(solution)/shard_map/ppermute | solution.py:414
  19.1 0.2 collective-permute-start.4
  19.2 2.2 %shard_map.47 = (f32[192,24]{1,0:T(8,128)S(1)}, f32[24,24]{1,0:T(8,128)S(1)}, bf16[24,8192]{1,0:T(8,128)(2,1)S(1)}, f32[8,64,128]{2,1,0:T(8,128)S(1)}) custom-call(bf16[192,8192]{1,0:T(8,128)(2,1)S(1)} %get-tuple-element.20.stack_ref.near_ref, f32[4,64,128]{2,1,0:T(8,128)S(1)} %get-tuple-element.24.order_ref.one_ref, f32[4,64,128]{2,1,0:T(8,128)S(1)} %get-tuple-element.25.two_ref), custom_call_target="tpu_custom_call" | custom-call | flops 1000000 | bytes 4194304 | tf_op jit(solution)/shard_map/pallas_call | solution.py:460
  21.6 4.3 %collective-permute-done.4.other_one_ref.here_one_ref = f32[4,64,128]{2,1,0:T(8,128)S(1)} collective-permute-done((f32[4,64,128]{2,1,0:T(8,128)S(1)}, f32[4,64,128]{2,1,0:T(8,128)S(1)}, u32[]{:S(2)}, u32[]{:S(2)}) %collective-permute-start.4) | collective-permute-done | bytes 131104 | tf_op jit(solution)/shard_map/ppermute | solution.py:414
  25.8 1.5 %shard_map.48 = (f32[16,128]{1,0:T(8,128)S(1)}, f32[16,128]{1,0:T(8,128)S(1)}) custom-call(bf16[192,8192]{1,0:T(8,128)(2,1)S(1)} %get-tuple-element.20.stack_ref.near_ref, f32[64,64]{1,0:T(8,128)S(1)} %get-tuple-element.21.order_ref.gram_ref, bf16[24,8192]{1,0:T(8,128)(2,1)S(1)} %get-tuple-element.26.pieces_ref, ...), custom_call_target="tpu_custom_call" | custom-call | flops 1000000 | bytes 1000000 | tf_op jit(solution)/shard_map/pallas_call | solution.py:468
  27.4 2.6 %collective-permute-start.6 = (f32[16,128]{1,0:T(8,128)S(1)}, f32[16,128]{1,0:T(8,128)S(1)}, u32[]{:S(2)}, u32[]{:S(2)}) collective-permute-start(f32[16,128]{1,0:T(8,128)S(1)} %get-tuple-element.32), channel_id=1, source_target_pairs={{0,16},{16,0},{1,17},{17,1},{2,18},{18,2},{3,19},{19,3},{4,20},{20... | collective-permute-start | bytes 24584 | tf_op jit(solution)/shard_map/ppermute | solution.py:414
  29.9 0.8 %collective-permute-done.6.two_ref = f32[16,128]{1,0:T(8,128)S(1)} collective-permute-done((f32[16,128]{1,0:T(8,128)S(1)}, f32[16,128]{1,0:T(8,128)S(1)}, u32[]{:S(2)}, u32[]{:S(2)}) %collective-permute-start.6) | collective-permute-done | bytes 8224 | tf_op jit(solution)/shard_map/ppermute | solution.py:414
  30.8 0.7 shard_map.49
  31.4 5.5 %all-to-all-start = ((f32[16,16,128]{2,1,0:T(8,128)}), f32[16,16,128]{2,1,0:T(8,128)S(1)}, u32[]{:S(2)}, u32[]{:S(2)}) async-start(f32[16,16,128]{2,1,0:T(8,128)} %shard_map.49), calls=%async_computation | async-start | bytes 262144 | tf_op jit(solution)/shard_map/all_to_all | solution.py:418
  37.0 2.9 %collective-permute-start.7 = (f32[8,64,128]{2,1,0:T(8,128)S(1)}, f32[8,64,128]{2,1,0:T(8,128)S(1)}, u32[]{:S(2)}, u32[]{:S(2)}) collective-permute-start(f32[8,64,128]{2,1,0:T(8,128)S(1)} %get-tuple-element.34.keep_ref), channel_id=1, source_target_pairs={{0,1},{1,0},{2,3},{3,2},{4,5},{5,4},{6,7},{7,6},{8,9},{9,8},{10,11... | collective-permute-start | bytes 786440 | tf_op jit(solution)/shard_map/ppermute | solution.py:414
  39.8 4.2 %all-to-all-done.parts_ref = f32[16,16,128]{2,1,0:T(8,128)S(1)} async-done(((f32[16,16,128]{2,1,0:T(8,128)}), f32[16,16,128]{2,1,0:T(8,128)S(1)}, u32[]{:S(2)}, u32[]{:S(2)}) %all-to-all-start) | async-done | bytes 131104 | tf_op jit(solution)/shard_map/all_to_all | solution.py:418
  44.1 20.3 %all_to_all.10.parts_ref = f32[16,16,128]{2,1,0:T(8,128)S(1)} all-to-all(f32[16,16,128]{2,1,0:T(8,128)S(1)} %shard_map.50), channel_id=1, replica_groups=mesh['pair'=8,'core'=2,'lat'=8,'tm'=2] {'core','lat'}, dimensions={0} | all-to-all | bytes 262144 | tf_op jit(solution)/shard_map/all_to_all | solution.py:418
  64.3 2.9 %shard_map.51 = (bf16[128,160]{1,0:T(8,128)(2,1)S(1)}, f32[8,64]{1,0:T(8,128)}) custom-call(f32[16,16,128]{2,1,0:T(8,128)S(1)} %all_to_all.10.parts_ref), custom_call_target="tpu_custom_call" | custom-call | flops 1000000 | bytes 1000000 | tf_op jit(solution)/shard_map/pallas_call | solution.py:476
  67.3 1.9 %copy-done.1 = bf16[192,8192]{1,0:T(8,128)(2,1)S(1)} copy-done((bf16[192,8192]{1,0:T(8,128)(2,1)S(1)}, bf16[192,8192]{1,0:T(8,128)(2,1)}, u32[]{:S(2)}) %copy-start.1) | copy-done | bytes 3145752
  69.2 2.4 %shard_map.52 = f32[64,128,128]{2,1,0:T(8,128)} custom-call(bf16[128,160]{1,0:T(8,128)(2,1)S(1)} %get-tuple-element.33.maps_ref, bf16[192,8192]{1,0:T(8,128)(2,1)S(1)} %copy-done.1, bf16[128,8192]{1,0:T(8,128)(2,1)S(1)} %shard_map.42.order_ref.far_ref, f32[8,64,128]{2,1,0:T(8,128)S(1)} %get-tuple-element.34.keep_ref, ...), custom_call_target="tpu_custom_call" | custom-call | tf_op jit(solution)/shard_map/pallas_call | solution.py:480
  (15 shorter events, 0.4 us)
Async XLA Ops:
  0.6 1.0 %copy-start.2 = (f32[8,8,16,128]{3,2,1,0:T(8,128)S(1)}, f32[8,8,16,128]{3,2,1,0:T(8,128)}, u32[]{:S(2)}) copy-start(f32[8,8,16,128]{3,2,1,0:T(8,128)} %x_ref.7) | copy-start | bytes 1572868
  1.7 7.2 %copy-start.3 = (f32[8,8,16,128]{3,2,1,0:T(8,128)S(1)}, f32[8,8,16,128]{3,2,1,0:T(8,128)}, u32[]{:S(2)}) copy-start(f32[8,8,16,128]{3,2,1,0:T(8,128)} %x_ref.7) | copy-start | bytes 1572868
  1.9 5.2 %collective-permute-start.1 = (f32[128,128]{1,0:T(8,128)S(1)}, f32[128,128]{1,0:T(8,128)S(1)}, u32[]{:S(2)}, u32[]{:S(2)}) collective-permute-start(f32[128,128]{1,0:T(8,128)S(1)} %shard_map.41.order_ref.packed_ref), channel_id=1, source_target_pairs={{0,16},{16,0},{1,17},{17,1},{2,18},{18,2},{3,19},{19,3},{4,20},{20... | collective-permute-start | bytes 196616 | tf_op jit(solution)/shard_map/ppermute | solution.py:414
  5.2 3.7 %collective-permute-start = (f32[128,128]{1,0:T(8,128)S(1)}, f32[128,128]{1,0:T(8,128)S(1)}, u32[]{:S(2)}, u32[]{:S(2)}) collective-permute-start(f32[128,128]{1,0:T(8,128)S(1)} %shard_map.41.order_ref.packed_ref), channel_id=1, source_target_pairs={{16,32},{32,16},{48,64},{64,48},{80,96},{96,80},{112,128},{128,112... | collective-permute-start | bytes 196616 | tf_op jit(solution)/shard_map/ppermute | solution.py:410
  9.0 4.4 %collective-permute-start.2 = (f32[27,8,128]{2,1,0:T(8,128)S(1)}, f32[27,8,128]{2,1,0:T(8,128)S(1)}, u32[]{:S(2)}, u32[]{:S(2)}) collective-permute-start(f32[27,8,128]{2,1,0:T(8,128)S(1)} %get-tuple-element.22), channel_id=1, source_target_pairs={{0,2},{2,0},{4,6},{6,4},{8,10},{10,8},{12,14},{14,12},{1,3},{3,1},... | collective-permute-start | bytes 331784 | tf_op jit(solution)/shard_map/ppermute | solution.py:410
  9.1 4.3 %collective-permute-start.3 = (f32[27,8,128]{2,1,0:T(8,128)S(1)}, f32[27,8,128]{2,1,0:T(8,128)S(1)}, u32[]{:S(2)}, u32[]{:S(2)}) collective-permute-start(f32[27,8,128]{2,1,0:T(8,128)S(1)} %get-tuple-element.23), channel_id=1, source_target_pairs={{2,4},{4,2},{6,8},{8,6},{10,12},{12,10},{3,5},{5,3},{7,9},{9,7},{1... | collective-permute-start | bytes 331784 | tf_op jit(solution)/shard_map/ppermute | solution.py:410
  13.3 14.0 %copy-start = (bf16[192,8192]{1,0:T(8,128)(2,1)}, bf16[192,8192]{1,0:T(8,128)(2,1)S(1)}, u32[]{:S(2)}) copy-start(bf16[192,8192]{1,0:T(8,128)(2,1)S(1)} %get-tuple-element.20.stack_ref.near_ref) | copy-start | bytes 9437188
  16.2 5.4 %collective-permute-start.5 = (f32[4,64,128]{2,1,0:T(8,128)S(1)}, f32[4,64,128]{2,1,0:T(8,128)S(1)}, u32[]{:S(2)}, u32[]{:S(2)}) collective-permute-start(f32[4,64,128]{2,1,0:T(8,128)S(1)} %get-tuple-element.28.send_two_ref), channel_id=1, source_target_pairs={{0,1},{1,0},{2,3},{3,2},{4,5},{5,4},{6,7},{7,6},{8,9},{9,8},{10,11... | collective-permute-start | bytes 393224 | tf_op jit(solution)/shard_map/ppermute | solution.py:414
  19.1 6.8 %collective-permute-start.4 = (f32[4,64,128]{2,1,0:T(8,128)S(1)}, f32[4,64,128]{2,1,0:T(8,128)S(1)}, u32[]{:S(2)}, u32[]{:S(2)}) collective-permute-start(f32[4,64,128]{2,1,0:T(8,128)S(1)} %get-tuple-element.27.send_one_ref), channel_id=1, source_target_pairs={{0,1},{1,0},{2,3},{3,2},{4,5},{5,4},{6,7},{7,6},{8,9},{9,8},{10,11... | collective-permute-start | bytes 393224 | tf_op jit(solution)/shard_map/ppermute | solution.py:414
  27.4 3.4 %collective-permute-start.6 = (f32[16,128]{1,0:T(8,128)S(1)}, f32[16,128]{1,0:T(8,128)S(1)}, u32[]{:S(2)}, u32[]{:S(2)}) collective-permute-start(f32[16,128]{1,0:T(8,128)S(1)} %get-tuple-element.32), channel_id=1, source_target_pairs={{0,16},{16,0},{1,17},{17,1},{2,18},{18,2},{3,19},{19,3},{4,20},{20... | collective-permute-start | bytes 24584 | tf_op jit(solution)/shard_map/ppermute | solution.py:414
  31.4 12.6 %all-to-all-start = ((f32[16,16,128]{2,1,0:T(8,128)}), f32[16,16,128]{2,1,0:T(8,128)S(1)}, u32[]{:S(2)}, u32[]{:S(2)}) async-start(f32[16,16,128]{2,1,0:T(8,128)} %shard_map.49), calls=%async_computation | async-start | bytes 262144 | tf_op jit(solution)/shard_map/all_to_all | solution.py:418
  37.0 30.3 %collective-permute-start.7 = (f32[8,64,128]{2,1,0:T(8,128)S(1)}, f32[8,64,128]{2,1,0:T(8,128)S(1)}, u32[]{:S(2)}, u32[]{:S(2)}) collective-permute-start(f32[8,64,128]{2,1,0:T(8,128)S(1)} %get-tuple-element.34.keep_ref), channel_id=1, source_target_pairs={{0,1},{1,0},{2,3},{3,2},{4,5},{5,4},{6,7},{7,6},{8,9},{9,8},{10,11... | collective-permute-start | bytes 786440 | tf_op jit(solution)/shard_map/ppermute | solution.py:414
  67.3 1.9 %copy-start.1 = (bf16[192,8192]{1,0:T(8,128)(2,1)S(1)}, bf16[192,8192]{1,0:T(8,128)(2,1)}, u32[]{:S(2)}) copy-start(bf16[192,8192]{1,0:T(8,128)(2,1)} %copy-done) | copy-start | bytes 9437188
